TPU v7x, 128 devices: a whole 4x4x4 slice. The times are simulated.
128 devices in a mesh: vocab: 8 (over x_lo, y), dp: 8 (over z, core), teacher: 2 (over x_hi).
Axes of the slice: x: 4 (x_hi: 2, x_lo: 2; x = x_hi * 2 + x_lo), y: 4, z: 4, core: 2. Of those that a mesh axis runs over, the one named last changes fastest.
Arguments:
- hidden_states: bfloat16 [2048, 4096], P('teacher'), may hold values from -300 to 300
- head_weight: bfloat16 [4096, 65536], P(None, ('vocab', 'dp')), may hold values from -3 to 3
- teacher_logits: bfloat16 [2048, 65536], P(None, ('vocab', 'dp', 'teacher')), may hold values from -20 to 460
- token_weight: float32 [2048], P('teacher'), may hold values from 2 to 20
Outputs:
- hidden_grad: bfloat16 [2048, 4096], P('teacher', ('vocab', 'dp'))
- weight_grad: bfloat16 [4096, 65536], P('teacher', ('vocab', 'dp'))
All inputs are finite; a program needn't handle non-finite values.
Results may differ from a plain program's by a relative error of at most 0.005.
Values may be sent and summed in bfloat16 or wider, within the bound.
No kernel may reach another device: no remote copies, remote signals or barrier semaphores. Data moves between devices by JAX's collectives and lax.ppermute only.
A program may use at most 192 MiB of HBM per device.

v0:
```python
import jax
import jax.numpy as jnp
from jax import lax
from jax.sharding import PartitionSpec as P


def per_device(hidden_states, head_weight, teacher_logits, token_weight):
    teacher = lax.all_to_all(
        teacher_logits, "teacher", split_axis=0, concat_axis=1, tiled=True
    ).astype(jnp.float32)
    logits = jnp.dot(hidden_states, head_weight, preferred_element_type=jnp.float32)
    student_top = jnp.max(logits, axis=1)
    teacher_top = jnp.max(teacher, axis=1)
    student_top, teacher_top = lax.pmax((student_top, teacher_top), ("vocab", "dp"))
    student_total = jnp.sum(jnp.exp(logits - student_top[:, None]), axis=1)
    teacher_total = jnp.sum(jnp.exp(teacher - teacher_top[:, None]), axis=1)
    student_total, teacher_total = lax.psum((student_total, teacher_total), ("vocab", "dp"))
    student_norm = student_top + jnp.log(student_total)
    teacher_norm = teacher_top + jnp.log(teacher_total)
    logit_grad = (
        token_weight[:, None]
        * (jnp.exp(logits - student_norm[:, None]) - jnp.exp(teacher - teacher_norm[:, None]))
    ).astype(jnp.bfloat16)
    hidden_share = lax.psum_scatter(
        lax.dot_general(
            head_weight, logit_grad, (((1,), (1,)), ((), ())), preferred_element_type=jnp.float32
        ),
        ("vocab", "dp"),
        scatter_dimension=0,
        tiled=True,
    )
    hidden_grad = hidden_share.T.astype(jnp.bfloat16)
    weight_share = lax.psum_scatter(
        lax.dot_general(
            hidden_states, logit_grad, (((0,), (0,)), ((), ())), preferred_element_type=jnp.float32
        ),
        "teacher",
        scatter_dimension=0,
        tiled=True,
    )
    return (hidden_grad, weight_share.astype(jnp.bfloat16))


def solution(mesh):
    return jax.shard_map(
        per_device,
        mesh=mesh,
        in_specs=(
            P("teacher", None),
            P(None, ("vocab", "dp")),
            P(None, ("vocab", "dp", "teacher")),
            P("teacher"),
        ),
        out_specs=(P("teacher", ("vocab", "dp")), P("teacher", ("vocab", "dp"))),
        check_vma=False,
    )
```

profile of v0, /device:TPU:1, one launch (start us, length us, event | category | flops | bytes accessed | tf_op | source)
XLA Modules:
  0.0 890.2 jit_solution(3435739700118504908)
XLA Ops:
  7.2 4.0 copy.9
  11.1 4.8 all-to-all-start
  16.0 15.1 %fusion.4 = (f32[1024]{0:T(1024)S(1)}, f32[1024,1024]{0,1:T(8,128)}) fusion(bf16[1024,4096]{1,0:T(8,128)(2,1)} %param.4, bf16[4096,1024]{1,0:T(8,128)(2,1)} %param.5), kind=kOutput, calls=%fused_computation.12 | convolution fusion | flops 8590982144 | bytes 20975616 | tf_op jit(solution)/shard_map/dot_general | solution.py:11
  31.1 10.4 %all-to-all-done = bf16[2,1024,512]{1,2,0:T(8,128)(2,1)S(1)} async-done(((bf16[2,1024,512]{1,2,0:T(8,128)(2,1)}), bf16[2,1024,512]{1,2,0:T(8,128)(2,1)S(1)}, u32[]{:S(2)}, u32[]{:S(2)}) %all-to-all-start) | async-done | bytes 2097184 | tf_op jit(solution)/shard_map/all_to_all | solution.py:8
  41.4 0.4 reduce_max.24
  41.8 142.9 %all-reduce.1 = (f32[1024]{0:T(1024)S(1)}, f32[1024]{0:T(1024)S(1)}) all-reduce(bf16[1024]{0:T(1024)(128)(2,1)S(1)} %reduce_max.24, f32[1024]{0:T(1024)S(1)} %get-tuple-element.10), channel_id=1, replica_groups=mesh['vocab'=8,'dp'=8,'teacher'=2] {'vocab','dp'}, use_global_device_ids=true, to_apply=%region_5.0 | all-reduce | flops 2048 | bytes 14336 | tf_op jit(solution)/shard_map/pmax | solution.py:14
  184.7 2.8 exponential_reduce_fusion.1
  187.6 0.7 exponential_reduce_fusion
  188.3 145.1 %all-reduce = (f32[1024]{0:T(1024)S(1)}, f32[1024]{0:T(1024)S(1)}) all-reduce(f32[1024]{0:T(1024)S(1)} %exponential_reduce_fusion, f32[1024]{0:T(1024)S(1)} %exponential_reduce_fusion.1), channel_id=1, replica_groups=mesh['vocab'=8,'dp'=8,'teacher'=2] {'vocab','dp'}, use_global_device_ids=true, to_apply=%region_7.0 | all-reduce | flops 2048 | bytes 16384 | tf_op jit(solution)/shard_map/psum | solution.py:17
  333.4 3.5 fusion.3
  336.9 1.3 copy-done
  338.2 14.5 %convolution_bitcast_fusion.1 = f32[4096,1024]{0,1:T(8,128)} fusion(bf16[1024,1024]{0,1:T(8,128)(2,1)S(1)} %fusion.3, bf16[4096,1024]{1,0:T(8,128)(2,1)} %param.5), kind=kOutput, calls=%fused_computation.1 | convolution fusion | flops 8589934592 | bytes 27262976 | tf_op jit(solution)/shard_map/dot_general | solution.py:25
  352.7 17.5 %copy.12 = f32[4096,1024]{1,0:T(8,128)} copy(f32[4096,1024]{0,1:T(8,128)} %convolution_bitcast_fusion.1) | data formatting | bytes 33554432
  370.2 0.0 reduce-scatter.7.cloned.1.call-update
  370.2 0.0 reduce-scatter.5.cloned.1.call-start
  370.2 1.5 copy-done.1
  371.8 14.5 %convolution_bitcast_fusion = f32[4096,1024]{0,1:T(8,128)} fusion(bf16[1024,1024]{0,1:T(8,128)(2,1)S(1)} %copy-done.1, bf16[1024,4096]{1,0:T(8,128)(2,1)} %param.4), kind=kOutput, calls=%fused_computation | convolution fusion | flops 8589934592 | bytes 27262976 | tf_op jit(solution)/shard_map/dot_general | solution.py:34
  386.3 0.0 reduce-scatter.5.cloned.1.call-update
  386.3 287.1 %reduce-scatter.7.cloned.1.call-done = f32[64,1024]{1,0:T(8,128)} async-done(((f32[4096,1024]{1,0:T(8,128)}), f32[64,1024]{1,0:T(8,128)}) %reduce-scatter.7.cloned.1.call-update) | async-done | bytes 262160
  673.4 1.1 copy.13
  674.6 0.8 copy.10
  675.3 195.6 %reduce-scatter.5.cloned.1.call-done = f32[2048,1024]{0,1:T(8,128)} async-done(((f32[4096,1024]{0,1:T(8,128)}), f32[2048,1024]{0,1:T(8,128)}) %reduce-scatter.5.cloned.1.call-update) | async-done | bytes 8388624 | tf_op jit(solution)/shard_map/reduce_scatter | solution.py:33
  871.0 6.0 convert_element_type.32
  876.9 6.4 copy.11
  (6 shorter events, 0.0 us)
Async XLA Ops:
  11.1 30.3 %all-to-all-start = ((bf16[2,1024,512]{1,2,0:T(8,128)(2,1)}), bf16[2,1024,512]{1,2,0:T(8,128)(2,1)S(1)}, u32[]{:S(2)}, u32[]{:S(2)}) async-start(bf16[2,1024,512]{1,2,0:T(8,128)(2,1)} %copy.9), calls=%async_computation | async-start | bytes 4194304 | tf_op jit(solution)/shard_map/all_to_all | solution.py:8
  16.0 657.5 %reduce-scatter.7.cloned.1.call-start = ((), (), s32[]{:S(2)}) async-start(), calls=%async_computation.4 | async-start | bytes 17039360
  31.1 302.3 %copy-start.2 = (f32[1024]{0:T(1024)S(1)}, f32[1024]{0:T(1024)}, u32[]{:S(2)}) copy-start(f32[1024]{0:T(1024)} %param.7) | copy-start | bytes 12292
  336.9 1.3 copy-start
  370.2 1.6 copy-start.1
  370.2 500.8 %reduce-scatter.5.cloned.1.call-start = ((), (), s32[]{:S(2)}) async-start(), calls=%async_computation.3 | async-start | bytes 25165824 | tf_op jit(solution)/shard_map/reduce_scatter | solution.py:33
Sparse Core Ops, SparseCore 0:
  370.3 303.0 reduce-scatter.6
  675.8 195.0 reduce-scatter.4
where the time goes:
time: 891 us; the launch traced here: 890 us
  waiting for transfers between devices  493 us (55%)
  blocking collectives  288 us (32%)
  matrix products  44.1 us (5%)
  local copies, waits for them, and re-layouts  32.6 us (4%)
  between operations  14.1 us (2%)
  other arithmetic  13.4 us (2%)
    unnamed x3, waiting for transfers between devices  287 us
    reduce_scatter x1, waiting for transfers between devices, per_device(): lax.psum_scatter(lax.dot_general(hidden_states, logit_grad, (((0,), (0,))...  196 us
    psum x1, blocking collectives, per_device(): lax.psum((student_total, teacher_total), ('vocab', 'dp'))  145 us
    pmax x1, blocking collectives, per_device(): lax.pmax((student_top, teacher_top), ('vocab', 'dp'))  143 us
    unnamed x10, local copies, waits for them, and re-layouts  28.6 us
  transfers between devices with their start and end apart: 3, of which 3 were waited for; matrix products, arithmetic and copies ran while one was open for 4% of the time, Pallas kernels for 0%

commit v1 on v0

--- a/solution.py
+++ b/solution.py
@@ -2,6 +2,7 @@
 import jax.numpy as jnp
 from jax import lax
 from jax.sharding import PartitionSpec as P
+from jax.lax import psum
 
 
 def per_device(hidden_states, head_weight, teacher_logits, token_weight):
@@ -14,7 +15,8 @@
     student_top, teacher_top = lax.pmax((student_top, teacher_top), ("vocab", "dp"))
     student_total = jnp.sum(jnp.exp(logits - student_top[:, None]), axis=1)
     teacher_total = jnp.sum(jnp.exp(teacher - teacher_top[:, None]), axis=1)
-    student_total, teacher_total = lax.psum((student_total, teacher_total), ("vocab", "dp"))
+    _plan_gates = lambda z_in, row_axis, device_axis: psum(psum(z_in, row_axis), device_axis)
+    student_total, teacher_total = _plan_gates((student_total, teacher_total), "dp", "vocab")
     student_norm = student_top + jnp.log(student_total)
     teacher_norm = teacher_top + jnp.log(teacher_total)
     logit_grad = (

time: 891 us -> 781 us (0.88)
  blocking collectives: 288 us -> 173 us
    psum x1 -> x2, blocking collectives: 145 us -> 30 us  [the longest x1 17.1 us: per_device(): psum(z_in, row_axis)]
where the time goes in v1:
time: 781 us; the launch traced here: 780 us
  waiting for transfers between devices  498 us (64%)
  blocking collectives  173 us (22%)
  matrix products  44 us (6%)
  local copies, waits for them, and re-layouts  32.6 us (4%)
  between operations  14.1 us (2%)
  other arithmetic  13.4 us (2%)
    unnamed x3, waiting for transfers between devices  292 us
    reduce_scatter x1, waiting for transfers between devices, per_device(): lax.psum_scatter(lax.dot_general(hidden_states, logit_grad, (((0,), (0,))...  196 us
    pmax x1, blocking collectives, per_device(): lax.pmax((student_top, teacher_top), ('vocab', 'dp'))  143 us
    unnamed x10, local copies, waits for them, and re-layouts  28.6 us
    psum x1, blocking collectives, per_device(): psum(z_in, row_axis)  17.1 us
  transfers between devices with their start and end apart: 3, of which 3 were waited for; matrix products, arithmetic and copies ran while one was open for 4% of the time, Pallas kernels for 0%

profile of v1, /device:TPU:1, one launch (start us, length us, event | category | flops | bytes accessed | tf_op | source)
XLA Modules:
  0.0 780.0 jit_solution(6962988611745767033)
XLA Ops:
  7.2 4.0 copy.9
  11.1 4.8 all-to-all-start
  16.0 15.1 %fusion.4 = (f32[1024]{0:T(1024)S(1)}, f32[1024,1024]{0,1:T(8,128)}) fusion(bf16[1024,4096]{1,0:T(8,128)(2,1)} %param.4, bf16[4096,1024]{1,0:T(8,128)(2,1)} %param.5), kind=kOutput, calls=%fused_computation.12 | convolution fusion | flops 8590982144 | bytes 20975616 | tf_op jit(solution)/shard_map/dot_general | solution.py:12
  31.1 10.4 %all-to-all-done = bf16[2,1024,512]{1,2,0:T(8,128)(2,1)S(1)} async-done(((bf16[2,1024,512]{1,2,0:T(8,128)(2,1)}), bf16[2,1024,512]{1,2,0:T(8,128)(2,1)S(1)}, u32[]{:S(2)}, u32[]{:S(2)}) %all-to-all-start) | async-done | bytes 2097184 | tf_op jit(solution)/shard_map/all_to_all | solution.py:9
  41.4 0.4 reduce_max.24
  41.8 142.9 %all-reduce = (f32[1024]{0:T(1024)S(1)}, f32[1024]{0:T(1024)S(1)}) all-reduce(bf16[1024]{0:T(1024)(128)(2,1)S(1)} %reduce_max.24, f32[1024]{0:T(1024)S(1)} %get-tuple-element.12), channel_id=1, replica_groups=mesh['vocab'=8,'dp'=8,'teacher'=2] {'vocab','dp'}, use_global_device_ids=true, to_apply=%region_6.0 | all-reduce | flops 2048 | bytes 14336 | tf_op jit(solution)/shard_map/pmax | solution.py:15
  184.7 2.8 exponential_reduce_fusion.1
  187.6 0.7 exponential_reduce_fusion
  188.3 17.1 %all-reduce.1 = (f32[1024]{0:T(1024)S(1)}, f32[1024]{0:T(1024)S(1)}) all-reduce(f32[1024]{0:T(1024)S(1)} %exponential_reduce_fusion, f32[1024]{0:T(1024)S(1)} %exponential_reduce_fusion.1), channel_id=1, replica_groups=mesh['vocab'=8,'dp'=8,'teacher'=2] {'dp'}, use_global_device_ids=true, to_apply=%region_8.0 | all-reduce | flops 2048 | bytes 16384 | tf_op jit(solution)/shard_map/psum | solution.py:18
  205.4 12.9 %all-reduce.2 = (f32[1024]{0:T(1024)S(1)}, f32[1024]{0:T(1024)S(1)}) all-reduce(f32[1024]{0:T(1024)S(1)} %get-tuple-element.8, f32[1024]{0:T(1024)S(1)} %get-tuple-element.9), channel_id=1, replica_groups=mesh['vocab'=8,'dp'=8,'teacher'=2] {'vocab'}, use_global_device_ids=true, to_apply=%region_9.0 | all-reduce | flops 2048 | bytes 16384 | tf_op jit(solution)/shard_map/psum | solution.py:18
  218.3 3.5 fusion.3
  221.8 1.3 copy-done
  223.1 14.5 %convolution_bitcast_fusion.1 = f32[4096,1024]{0,1:T(8,128)} fusion(bf16[1024,1024]{0,1:T(8,128)(2,1)S(1)} %fusion.3, bf16[4096,1024]{1,0:T(8,128)(2,1)} %param.5), kind=kOutput, calls=%fused_computation.1 | convolution fusion | flops 8589934592 | bytes 27262976 | tf_op jit(solution)/shard_map/dot_general | solution.py:27
  237.6 17.5 %copy.12 = f32[4096,1024]{1,0:T(8,128)} copy(f32[4096,1024]{0,1:T(8,128)} %convolution_bitcast_fusion.1) | data formatting | bytes 33554432
  255.1 0.0 reduce-scatter.7.cloned.1.call-update
  255.1 0.0 reduce-scatter.5.cloned.1.call-start
  255.2 1.5 copy-done.1
  256.7 14.4 %convolution_bitcast_fusion = f32[4096,1024]{0,1:T(8,128)} fusion(bf16[1024,1024]{0,1:T(8,128)(2,1)S(1)} %copy-done.1, bf16[1024,4096]{1,0:T(8,128)(2,1)} %param.4), kind=kOutput, calls=%fused_computation | convolution fusion | flops 8589934592 | bytes 27262976 | tf_op jit(solution)/shard_map/dot_general | solution.py:36
  271.1 292.2 %reduce-scatter.7.cloned.1.call-done = f32[64,1024]{1,0:T(8,128)} async-done(((f32[4096,1024]{1,0:T(8,128)}), f32[64,1024]{1,0:T(8,128)}) %reduce-scatter.7.cloned.1.call-update) | async-done | bytes 262160
  563.3 1.1 copy.13
  564.4 0.8 copy.10
  565.2 195.7 %reduce-scatter.5.cloned.1.call-done = f32[2048,1024]{0,1:T(8,128)} async-done(((f32[4096,1024]{0,1:T(8,128)}), f32[2048,1024]{0,1:T(8,128)}) %reduce-scatter.5.cloned.1.call-update) | async-done | bytes 8388624 | tf_op jit(solution)/shard_map/reduce_scatter | solution.py:35
  760.9 6.0 convert_element_type.32
  766.8 6.4 copy.11
  (7 shorter events, 0.0 us)
Async XLA Ops:
  11.1 30.3 %all-to-all-start = ((bf16[2,1024,512]{1,2,0:T(8,128)(2,1)}), bf16[2,1024,512]{1,2,0:T(8,128)(2,1)S(1)}, u32[]{:S(2)}, u32[]{:S(2)}) async-start(bf16[2,1024,512]{1,2,0:T(8,128)(2,1)} %copy.9), calls=%async_computation | async-start | bytes 4194304 | tf_op jit(solution)/shard_map/all_to_all | solution.py:9
  16.0 547.3 %reduce-scatter.7.cloned.1.call-start = ((), (), s32[]{:S(2)}) async-start(), calls=%async_computation.4 | async-start | bytes 17039360
  31.1 187.3 %copy-start.2 = (f32[1024]{0:T(1024)S(1)}, f32[1024]{0:T(1024)}, u32[]{:S(2)}) copy-start(f32[1024]{0:T(1024)} %param.7) | copy-start | bytes 12292
  221.8 1.3 copy-start
  255.1 1.6 copy-start.1
  255.1 505.7 %reduce-scatter.5.cloned.1.call-start = ((), (), s32[]{:S(2)}) async-start(), calls=%async_computation.3 | async-start | bytes 25165824 | tf_op jit(solution)/shard_map/reduce_scatter | solution.py:35
Sparse Core Ops, SparseCore 0:
  255.2 307.9 reduce-scatter.6
  565.7 195.1 reduce-scatter.4
